TPU v7x, 256 devices: a whole 4x4x8 slice. The times are simulated.
256 devices in a mesh: samples: 64 (over z, y, core), groups: 4 (over x).
Axes of the slice: x: 4, y: 4, z: 8, core: 2. Of those that a mesh axis runs over, the one named last changes fastest.
Arguments:
- observed: bfloat16 [1024, 81920], P('samples', 'groups'), may hold values from -200 to 200
- labels: int32 [81920], P('groups'), may hold values from 0 to 255, as said below
- comp_sizes: int32 [256], P('groups'), may hold values from 128 to 512, as said below
Outputs:
- whitened: bfloat16 [1024, 81920], P('samples', 'groups')
Inputs may be any that keep to these rules, and one draw needn't show every extreme that they name: Group g's columns (g * 20480 to (g + 1) * 20480 - 1) carry exactly the labels g * 64 to (g + 1) * 64 - 1, and label c stands on exactly comp_sizes[c] columns. `comp_sizes`: in every group one component has exactly 512 variables; components 2k and 2k + 1 (k = 0, 1, ...) together have exactly 640 variables.
All inputs are finite; a program needn't handle non-finite values. Where the computation divides by a largest or mean magnitude, that divisor is 1e-20 or more.
Results may differ from a plain program's by a relative error of at most 0.0038.
The roundings to bfloat16 on the way count: a program that leaves them out, or rounds other values in their place, can miss the bound.
Values may be sent and summed in bfloat16 or wider, within the bound.
No kernel may reach another device: no remote copies, remote signals or barrier semaphores. Data moves between devices by JAX's collectives and lax.ppermute only.
A program may use at most 64 MiB of HBM per device.

v0:
```python
import jax
import jax.numpy as jnp
from jax import lax
from jax.sharding import Mesh
from jax.sharding import PartitionSpec as P

CMAX = 512
ITERS = 5
SAMPLES = ("samples_0", "samples_1", "samples_2")
SAMPLES_GROUPS = ("samples_0", "samples_1", "samples_2", "groups")


shrink = 0.2
ridge = 0.5


def partner_2(x, axis, apart):
    return lax.ppermute(x, axis, [(i, i ^ 1 << apart) for i in range(lax.axis_size(axis))])


def one_axis_at_a_time(x, axes):
    for axis in axes:
        x = lax.psum(x, axis)
    return x


def newton_batch(matrices):
    extent = matrices.shape[-1]
    identity = jnp.eye(extent, dtype=jnp.float32)[None]
    row_bound = jnp.max(jnp.sum(jnp.abs(matrices), axis=2), axis=1)
    current = identity / row_bound[:, None, None]
    for sweep_index in range(ITERS):
        product = jnp.einsum("kab,kbc->kac", matrices, current, precision=lax.Precision.HIGHEST)
        current = jnp.einsum(
            "kab,kbc->kac", current, 2.0 * identity - product, precision=lax.Precision.HIGHEST
        )
    return current


def shrunk_inverse(covariance, slot_sizes, average):
    extent = covariance.shape[-1]
    target = jnp.trace(covariance, axis1=1, axis2=2) / slot_sizes.astype(jnp.float32)
    diag_lift = shrink * target + ridge * average
    matrices = (1.0 - shrink) * covariance + diag_lift[:, None, None] * jnp.eye(
        extent, dtype=jnp.float32
    )[None]
    return newton_batch(matrices).astype(jnp.bfloat16)


def body(observed, labels, comp_sizes):
    row_local, width_local = observed.shape
    slot_total = comp_sizes.shape[0]
    samples_count = lax.axis_size(SAMPLES)
    groups_count = lax.axis_size("groups")
    slot_here = slot_total // samples_count
    row_count = row_local * samples_count
    local_label = labels - lax.axis_index("groups") * slot_total
    sort_order = jnp.argsort(local_label, stable=True)
    slot_sizes = lax.dynamic_slice_in_dim(
        comp_sizes, lax.axis_index(SAMPLES) * slot_here, slot_here
    )
    own_slot = lax.axis_index(SAMPLES)
    half_index = own_slot % 2
    lead_size = comp_sizes[own_slot - half_index]
    own_size = comp_sizes[own_slot]
    own_start = jnp.where(half_index == 0, 0, lead_size)
    other_start = jnp.where(half_index == 0, lead_size, 0)
    valid = jnp.arange(CMAX, dtype=jnp.int32) < own_size
    valid_pairs = valid[:, None] & valid[None, :]
    bin_width = 2 * (width_local // slot_total)
    pair_total = slot_total // 2
    half_rows = row_local // 2
    tight = observed[:, sort_order]
    split_rows = tight.reshape(2, half_rows, pair_total, bin_width).transpose(1, 2, 0, 3)
    split_rows = split_rows.reshape(half_rows, slot_total, bin_width)
    received = lax.all_to_all(split_rows, SAMPLES, split_axis=1, concat_axis=0, tiled=True)
    bin_rows = received[:, 0, :]
    partial_value = jnp.dot(bin_rows.T, bin_rows, preferred_element_type=jnp.float32)
    bin_gram = partial_value + partner_2(partial_value, SAMPLES, 0)
    widened = jnp.pad(bin_gram, ((0, CMAX), (0, CMAX)))
    block = lax.dynamic_slice(widened, (own_start, own_start), (CMAX, CMAX))
    raw_sums = (block * valid_pairs.astype(jnp.float32))[None]
    energy = one_axis_at_a_time(jnp.sum(jnp.trace(raw_sums, axis1=1, axis2=2)), SAMPLES_GROUPS)
    average = energy / (row_count * width_local * groups_count)
    inverse = shrunk_inverse(raw_sums / row_count, slot_sizes, average)
    kept = jnp.where(valid_pairs, inverse[0], jnp.zeros_like(inverse[0]))
    partner = partner_2(kept, SAMPLES, 0)
    empty_canvas = jnp.zeros((bin_width + CMAX, bin_width + CMAX), jnp.bfloat16)
    own_canvas = lax.dynamic_update_slice(empty_canvas, kept, (own_start, own_start))
    other_canvas = lax.dynamic_update_slice(empty_canvas, partner, (other_start, other_start))
    block_diag = (own_canvas + other_canvas)[:bin_width, :bin_width]
    mapped = jnp.dot(bin_rows, block_diag, preferred_element_type=jnp.float32).astype(jnp.bfloat16)
    returned = lax.all_to_all(mapped[:, None, :], SAMPLES, split_axis=0, concat_axis=1, tiled=True)
    ordered = returned.reshape(half_rows, pair_total, 2, bin_width).transpose(2, 0, 1, 3)
    ordered = ordered.reshape(row_local, width_local)
    rank = (
        jnp.zeros((width_local,), jnp.int32)
        .at[sort_order]
        .set(jnp.arange(width_local, dtype=jnp.int32))
    )
    return jnp.take(ordered, rank, axis=1)


def solution(mesh):
    finer = Mesh(
        mesh.devices.reshape(8, 4, 2, mesh.shape["groups"]),
        ("samples_0", "samples_1", "samples_2", "groups"),
    )
    in_specs = (P(SAMPLES, "groups"), P("groups"), P("groups"))
    out_specs = P(SAMPLES, "groups")
    return jax.shard_map(body, mesh=finer, in_specs=in_specs, out_specs=out_specs, check_vma=False)
```

profile of v0, /device:TPU:1, one launch (start us, length us, event | category | flops | bytes accessed | tf_op | source)
XLA Modules:
  0.0 423.5 jit_solution(10780282538974206855)
XLA Ops:
  0.9 11.2 %sort.17 = (s32[20480]{0:T(1024)}, s32[20480]{0:T(1024)S(1)}) sort(s32[20480]{0:T(1024)S(1)} %broadcast_subtract_fusion, s32[20480]{0:T(1024)S(1)} %iota.72), dimensions={0}, to_apply=%region_0.0 | sort | flops 307200 | bytes 327680 | tf_op jit(solution)/shard_map/jit(argsort)/sort | solution.py:58
  12.2 5.0 %copy.43 = bf16[16,20480]{0,1:T(8,128)(2,1)} copy(bf16[16,20480]{1,0:T(8,128)(2,1)} %param.3) | data formatting | bytes 1310720 | tf_op args[0]
  17.2 71.8 %gather_fusion = bf16[20480,16]{1,0:T(8,128)(2,1)} fusion(bf16[16,20480]{0,1:T(8,128)(2,1)} %copy.43, s32[20480]{0:T(1024)S(1)} %get-tuple-element.10), kind=kCustom, calls=%fused_computation | custom fusion | bytes 1392640 | tf_op jit(solution)/shard_map/gather | solution.py:73
  89.0 3.9 copy.44
  93.2 33.3 %all_to_all.30 = bf16[8,64,640]{2,0,1:T(8,128)(2,1)S(1)} all-to-all(bf16[8,64,640]{2,0,1:T(8,128)(2,1)S(1)} %bitcast.60), channel_id=1, replica_groups=mesh['samples_0'=8,'samples_1'=4,'samples_2'=2,'groups'=4] {'samples_0',..., dimensions={1} | all-to-all | bytes 1310720 | tf_op jit(solution)/shard_map/all_to_all | solution.py:76
  134.2 12.7 %psum.28 = f32[]{:T(128)} all-reduce(f32[]{:T(128)} %get-tuple-element.7), channel_id=1, replica_groups=mesh['samples_0'=8,'samples_1'=4,'samples_2'=2,'groups'=4] {'samples_0'}, use_global_device_ids=true, to_apply=%region_4.5 | all-reduce | flops 1 | bytes 8 | tf_op jit(solution)/shard_map/psum | solution.py:23
  146.9 8.2 %psum.29 = f32[]{:T(128)} all-reduce(f32[]{:T(128)} %psum.28), channel_id=1, replica_groups=mesh['samples_0'=8,'samples_1'=4,'samples_2'=2,'groups'=4] {'samples_1'}, use_global_device_ids=true, to_apply=%region_5.6 | all-reduce | flops 1 | bytes 8 | tf_op jit(solution)/shard_map/psum | solution.py:23
  155.0 8.9 %psum.30 = f32[]{:T(128)} all-reduce(f32[]{:T(128)} %psum.29), channel_id=1, replica_groups=mesh['samples_0'=8,'samples_1'=4,'samples_2'=2,'groups'=4] {'samples_2'}, use_global_device_ids=true, to_apply=%region_6.7 | all-reduce | flops 1 | bytes 8 | tf_op jit(solution)/shard_map/psum | solution.py:23
  164.6 9.0 %psum.31 = f32[]{:T(128)} all-reduce(f32[]{:T(128)} %psum.30), channel_id=1, replica_groups=mesh['samples_0'=8,'samples_1'=4,'samples_2'=2,'groups'=4] {'groups'}, use_global_device_ids=true, to_apply=%region_7.8 | all-reduce | flops 1 | bytes 8 | tf_op jit(solution)/shard_map/psum | solution.py:23
  181.2 2.6 select_subtract_fusion.3
  185.6 2.6 select_subtract_fusion.2
  190.5 2.6 select_subtract_fusion.1
  195.0 2.6 select_subtract_fusion
  199.5 2.4 collective-permute-start.1
  202.5 75.5 %scatter_custom_fusion = s32[20480]{0:T(1024)S(1)} fusion(s32[20480]{0:T(1024)S(1)} %get-tuple-element.9, s32[20480]{0:T(1024)S(1)} %iota.73, s32[]{:T(128)} %constant.68.clone.1), kind=kCustom, calls=%fused_computation.44 | custom fusion | bytes 81924 | tf_op jit(solution)/shard_map/scatter | solution.py:99
  279.1 8.3 %dynamic_update_slice.8 = bf16[1152,1152]{0,1:T(8,128)(2,1)S(1)} dynamic-update-slice(bf16[1152,1152]{0,1:T(8,128)(2,1)S(1)} %broadcast_in_dim.41, bf16[512,512]{0,1:T(8,128)(2,1)S(1)} %and_select_fusion, s32[]{:T(128)S(6)} %select_n.65, s32[]{:T(128)S(6)} %select_n.65) | dynamic-update-slice | bytes 1048580 | tf_op jit(solution)/shard_map/dynamic_update_slice | solution.py:89
  288.7 7.5 %add.79 = bf16[1152,1152]{0,1:T(8,128)(2,1)S(1)} dynamic-update-slice(bf16[1152,1152]{0,1:T(8,128)(2,1)S(1)} %dynamic_update_slice.8, bf16[512,512]{0,1:T(8,128)(2,1)S(1)} %dynamic-slice_add_fusion, s32[]{:T(128)S(6)} %select_n.70, s32[]{:T(128)S(6)} %select_n.70) | dynamic-update-slice | bytes 1048580 | tf_op jit(solution)/shard_map/add | solution.py:91
  296.2 2.8 fusion.6
  302.9 6.4 %all-to-all-start.1 = ((bf16[64,2,2560]{2,1,0:T(2,128)(2,1)}), bf16[64,2,2560]{2,1,0:T(2,128)(2,1)S(1)}, u32[]{:S(2)}, u32[]{:S(2)}) async-start(bf16[64,2,2560]{2,1,0:T(2,128)(2,1)} %reshape.145), calls=%async_computation.1 | async-start | bytes 1310720 | tf_op jit(solution)/shard_map/all_to_all | solution.py:93
  309.3 20.3 %all-to-all-done.1 = bf16[64,2,2560]{2,1,0:T(2,128)(2,1)S(1)} async-done(((bf16[64,2,2560]{2,1,0:T(2,128)(2,1)}), bf16[64,2,2560]{2,1,0:T(2,128)(2,1)S(1)}, u32[]{:S(2)}, u32[]{:S(2)}) %all-to-all-start.1) | async-done | bytes 655392 | tf_op jit(solution)/shard_map/all_to_all | solution.py:93
  330.6 3.5 copy.56
  334.1 71.8 %gather_fusion.1 = bf16[20480,16]{1,0:T(8,128)(2,1)} fusion(bf16[16,20480]{0,1:T(8,128)(2,1)} %copy.56, s32[20480]{0:T(1024)S(1)} %fusion.16), kind=kCustom, calls=%fused_computation.1 | custom fusion | bytes 1392640 | tf_op jit(solution)/shard_map/jit(_take)/gather | solution.py:101
  405.9 12.5 %select_bitcast_fusion = bf16[16,20480]{0,1:T(8,128)(2,1)} fusion(bf16[20480,16]{1,0:T(8,128)(2,1)} %gather_fusion.1, pred[20480]{0:T(1024)(128)(4,1)S(1)} %compare_and_fusion), kind=kLoop, calls=%fused_computation.4 | loop fusion | flops 327680 | bytes 1331200 | tf_op jit(solution)/shard_map/jit(_take)/select_n | solution.py:101
  418.5 4.8 %copy.57 = bf16[16,20480]{1,0:T(8,128)(2,1)} copy(bf16[16,20480]{0,1:T(8,128)(2,1)} %select_bitcast_fusion) | data formatting | bytes 1310720 | tf_op jit(solution)/shard_map/jit(_take)/select_n | solution.py:101
  (38 shorter events, 29.0 us)
Async XLA Ops:
  92.9 34.9 %copy-start.1 = (s32[64]{0:T(128)S(1)}, s32[64]{0:T(128)}, u32[]{:S(2)}) copy-start(s32[64]{0:T(128)} %param.5) | copy-start | bytes 772
  127.2 2.5 copy-start
  127.2 3.9 collective-permute-start
  199.5 87.9 %collective-permute-start.1 = (bf16[512,512]{0,1:T(8,128)(2,1)S(1)}, bf16[512,512]{0,1:T(8,128)(2,1)}, u32[]{:S(2)}, u32[]{:S(2)}) collective-permute-start(bf16[512,512]{0,1:T(8,128)(2,1)S(1)} %and_select_fusion), channel_id=1, source_target_pairs={{0,4},{4,0},{8,12},{12,8},{16,20},{20,16},{24,28},{28,24},{32,36},... | collective-permute-start | bytes 1572872 | tf_op jit(solution)/shard_map/ppermute | solution.py:18
  302.9 26.8 %all-to-all-start.1 = ((bf16[64,2,2560]{2,1,0:T(2,128)(2,1)}), bf16[64,2,2560]{2,1,0:T(2,128)(2,1)S(1)}, u32[]{:S(2)}, u32[]{:S(2)}) async-start(bf16[64,2,2560]{2,1,0:T(2,128)(2,1)} %reshape.145), calls=%async_computation.1 | async-start | bytes 1310720 | tf_op jit(solution)/shard_map/all_to_all | solution.py:93
where the time goes:
time: 432 us; the launch traced here: 423 us
  local copies, waits for them, and re-layouts  257 us (59%)
  blocking collectives  72 us (17%)
  other arithmetic  33.3 us (8%)
  matrix products  26 us (6%)
  waiting for transfers between devices  21.7 us (5%)
  starting transfers between devices  9.47 us (2%)
  between operations  4.33 us (1%)
    gather x2, local copies, waits for them, and re-layouts, body(): tight = observed[:, sort_order]  75.7 us
    scatter x1, local copies, waits for them, and re-layouts, body(): rank = jnp.zeros((width_local,), jnp.int32).at[sort_order].set(jnp.arange...  75.5 us
    gather x1, local copies, waits for them, and re-layouts, body(): return jnp.take(ordered, rank, axis=1)  71.8 us
    psum x4, blocking collectives, one_axis_at_a_time(): x = lax.psum(x, axis)  38.7 us
    all_to_all x1, blocking collectives, body(): lax.all_to_all(split_rows, SAMPLES, split_axis=1, concat_axis=0, tiled=True)  33.3 us
    all_to_all x1, waiting for transfers between devices, body(): lax.all_to_all(mapped[:, None, :], SAMPLES, split_axis=0, concat_axis=1,...  20.3 us
    dot_general x5, matrix products, newton_batch(): jnp.einsum('kab,kbc->kac', matrices, current, precision=lax.Precision.HIG...  12.6 us
    select_n x1, other arithmetic, body(): return jnp.take(ordered, rank, axis=1)  12.5 us
  transfers between devices with their start and end apart: 3, of which 2 were waited for; matrix products, arithmetic and copies ran while one was open for 20% of the time, Pallas kernels for 0%

commit v1 on v0

v1 whole, which is shorter than its diff:
```python
import functools

import jax
import jax.numpy as jnp
from jax import lax
from jax.experimental import pallas as pl
from jax.experimental.pallas import tpu as pltpu
from jax.sharding import Mesh
from jax.sharding import PartitionSpec as P

CMAX = 512
ITERS = 5
LO = 256
LANES = 128
SAMPLES = ("samples_0", "samples_1", "samples_2")
BF16 = jnp.bfloat16
F32 = jnp.float32

shrink = 0.2
ridge = 0.5


def iota(shape, axis):
    return lax.broadcasted_iota(jnp.int32, shape, axis)


def dot(a, b, contract=((1,), (0,))):
    return lax.dot_general(a, b, (contract, ((), ())), preferred_element_type=F32)


def halves(x):
    top = x.astype(BF16)
    return top, (x - top.astype(F32)).astype(BF16)


def partition_kernel(sizes_ref, labels_ref, x_ref, out_ref, rank_ref, lhs_ref, acc_ref, base_ref, energy_ref):
    rows, chunk = x_ref.shape
    comps = sizes_ref.shape[1]
    his = acc_ref.shape[0] // rows
    units = his * LO // (comps // 2) // LANES
    step = pl.program_id(0)

    @pl.when(step == 0)
    def _():
        slot = iota((comps, comps), 0)
        before = (iota((comps, comps), 1) == slot - 1) & (slot % 2 == 1)
        sizes = jnp.broadcast_to(sizes_ref[...], (comps, comps))
        lead = jnp.sum(jnp.where(before, sizes, 0).astype(F32), axis=1, keepdims=True)
        first = iota((comps, LO), 0) // 2 * (units * LANES)
        base_ref[...] = first.astype(F32) + jnp.broadcast_to(lead, (comps, LO))
        acc_ref[...] = jnp.zeros_like(acc_ref)
        energy_ref[...] = jnp.zeros_like(energy_ref)

    upper = jnp.where(iota((LO, LO), 0) < iota((LO, LO), 1), 1.0, 0.0).astype(BF16)
    base = base_ref[...]
    ranks = []
    for tile in range(chunk // LO):
        label = labels_ref[:, tile * LO : (tile + 1) * LO] % comps
        hot = jnp.where(iota((comps, LO), 0) == label, 1.0, 0.0)
        count = dot(hot.astype(BF16), upper)
        ranks.append(jnp.sum(hot * (base + count), axis=0, keepdims=True))
        base = base + (count[:, LO - 1 :] + hot[:, LO - 1 :])
    base_ref[...] = base
    rank = jnp.concatenate(ranks, axis=1).astype(jnp.int32)
    rank_ref[...] = rank
    hi = rank // LO
    lo = rank - hi * LO
    x = x_ref[...]
    wide = x.astype(F32)
    square = wide * wide
    energy_ref[...] += sum(
        square[r * 8 : (r + 1) * 8, c * LANES : (c + 1) * LANES]
        for r in range(rows // 8)
        for c in range(chunk // LANES)
    )
    hi_rows = jnp.broadcast_to(hi.astype(F32), (rows, chunk)).astype(BF16)
    for h in range(his):
        lhs_ref[h * rows : (h + 1) * rows, :] = jnp.where(
            hi_rows == jnp.asarray(h, BF16), x, jnp.zeros_like(x)
        )
    lo_hot = jnp.where(iota((LO, chunk), 0) == lo, 1.0, 0.0).astype(BF16)
    acc_ref[...] += dot(lhs_ref[...], lo_hot, ((1,), (1,)))

    @pl.when(step == pl.num_programs(0) - 1)
    def _():
        total = jnp.sum(jnp.sum(energy_ref[...], axis=0, keepdims=True), axis=1, keepdims=True)
        first = total.astype(BF16).astype(F32)
        second = (total - first).astype(BF16).astype(F32)
        third = total - first - second
        row = iota((8, LANES), 0)
        pieces = jnp.where(row == 0, first, jnp.where(row == 1, second, jnp.where(row == 2, third, 0.0)))
        pieces = pieces.astype(BF16)
        for slot in range(comps):
            pair, half = divmod(slot, 2)
            for u in range(units):
                h, side = divmod(pair * units + u, LO // LANES)
                start = h * rows + half * 8
                value = acc_ref[start : start + 8, side * LANES : (side + 1) * LANES]
                out_ref[slot, :, u * LANES : (u + 1) * LANES] = value.astype(BF16)
            out_ref[slot, :, units * LANES :] = pieces


def partition(sizes, labels, x, chunk=2048):
    rows, width = x.shape
    comps = sizes.shape[0]
    his = width // LO
    message = 2 * width // comps + LANES
    return pl.pallas_call(
        partition_kernel,
        grid=(width // chunk,),
        in_specs=[
            pl.BlockSpec((1, comps), lambda i: (0, 0)),
            pl.BlockSpec((1, chunk), lambda i: (0, i)),
            pl.BlockSpec((rows, chunk), lambda i: (0, i)),
        ],
        out_specs=[
            pl.BlockSpec((comps, rows // 2, message), lambda i: (0, 0, 0)),
            pl.BlockSpec((1, chunk), lambda i: (0, i)),
        ],
        out_shape=[
            jax.ShapeDtypeStruct((comps, rows // 2, message), BF16),
            jax.ShapeDtypeStruct((1, width), jnp.int32),
        ],
        scratch_shapes=[
            pltpu.VMEM((rows * his, chunk), BF16),
            pltpu.VMEM((rows * his, LO), F32),
            pltpu.VMEM((comps, LO), F32),
            pltpu.VMEM((8, LANES), F32),
        ],
        compiler_params=pltpu.CompilerParams(vmem_limit_bytes=48 << 20),
        name="partition",
    )(sizes.reshape(1, comps), labels.reshape(1, width), x)


def product(a, b):
    return dot(a[0], b[0]) + (dot(a[0], b[1]) + dot(a[1], b[0]))


def inverse_kernel(slot_ref, sizes_ref, energy_ref, own_ref, other_ref, out_ref, *, entries):
    rows = own_ref.shape[0]
    slot = slot_ref[0]
    half = slot % 2
    lead = sizes_ref[slot - half]
    bin_width = CMAX + LANES
    size = jnp.where(half == 0, lead, bin_width - lead)
    begin = jnp.where(half == 0, 0, lead - LANES)
    end = jnp.where(half == 0, lead, CMAX)
    place = iota((1, CMAX), 1)
    live = (place >= begin) & (place < end)
    frame = pl.ds(pl.multiple_of(half * LANES, LANES), CMAX)
    live_rows = jnp.broadcast_to(jnp.where(live, 1.0, 0.0), (rows, CMAX)).astype(BF16)
    own = own_ref[:, frame] * live_rows
    other = other_ref[:, frame] * live_rows
    gram = dot(own, own, ((0,), (0,))) + dot(other, other, ((0,), (0,)))
    covariance = gram * (1.0 / (2 * rows))
    diagonal = iota((CMAX, CMAX), 0) == iota((CMAX, CMAX), 1)

    def whole(value, reduce):
        return reduce(reduce(value, axis=0, keepdims=True), axis=1, keepdims=True)

    trace = whole(jnp.where(diagonal, covariance, 0.0), jnp.sum)
    average = jnp.max(energy_ref[...], axis=1, keepdims=True) * (1.0 / entries)
    lift = shrink * (trace / jnp.full((1, 1), size.astype(F32))) + ridge * average
    matrix = (1.0 - shrink) * covariance + jnp.where(diagonal, lift, 0.0)
    bound = whole(jnp.sum(jnp.abs(matrix), axis=0, keepdims=True), jnp.max)
    scale = 1.0 / bound
    error = jnp.where(diagonal, 1.0, 0.0) - matrix * scale
    total = jnp.where(diagonal, 1.0, 0.0) + error
    for _ in range(ITERS - 1):
        parts = halves(error)
        error = product(parts, parts)
        total = total + product(halves(total), halves(error))
    inverse = jnp.where(live, total * scale, 0.0)
    keep = jnp.broadcast_to(jnp.where(live, 1.0, 0.0), (8, CMAX))
    keep = jnp.sum(jnp.where(diagonal, keep[:1], 0.0), axis=1, keepdims=True)
    out_ref[...] = (inverse * keep).astype(BF16)


def component_inverse(slot, sizes, energy, own, other, entries):
    bin_width = CMAX + LANES
    rows = own.shape[0]
    vmem = pl.BlockSpec((rows, bin_width), lambda i: (0, 0))
    return pl.pallas_call(
        functools.partial(inverse_kernel, entries=entries),
        grid=(1,),
        in_specs=[
            pl.BlockSpec(memory_space=pltpu.SMEM),
            pl.BlockSpec(memory_space=pltpu.SMEM),
            pl.BlockSpec((1, LANES), lambda i: (0, 0)),
            vmem,
            vmem,
        ],
        out_specs=pl.BlockSpec((CMAX, CMAX), lambda i: (0, 0)),
        out_shape=jax.ShapeDtypeStruct((CMAX, CMAX), BF16),
        compiler_params=pltpu.CompilerParams(vmem_limit_bytes=48 << 20),
        name="component_inverse",
    )(slot, sizes, energy, own, other)


def whiten_kernel(slot_ref, rows_ref, own_ref, other_ref, out_ref):
    swap = slot_ref[0] % 2 == 1
    own = own_ref[...]
    other = other_ref[...]
    lead = jnp.where(swap, other, own)
    tail = jnp.where(swap, own, other)
    first = dot(rows_ref[:, :CMAX], lead)
    second = dot(rows_ref[:, LANES:], tail)
    out_ref[:, :LANES] = first[:, :LANES].astype(BF16)
    out_ref[:, LANES:CMAX] = (first[:, LANES:] + second[:, : CMAX - LANES]).astype(BF16)
    out_ref[:, CMAX:] = second[:, CMAX - LANES :].astype(BF16)


def whiten(slot, rows, own, other):
    bin_width = CMAX + LANES
    count = rows.shape[0]
    square = pl.BlockSpec((CMAX, CMAX), lambda i: (0, 0))
    return pl.pallas_call(
        whiten_kernel,
        grid=(1,),
        in_specs=[
            pl.BlockSpec(memory_space=pltpu.SMEM),
            pl.BlockSpec((count, bin_width), lambda i: (0, 0)),
            square,
            square,
        ],
        out_specs=pl.BlockSpec((count, bin_width), lambda i: (0, 0)),
        out_shape=jax.ShapeDtypeStruct((count, bin_width), BF16),
        compiler_params=pltpu.CompilerParams(vmem_limit_bytes=48 << 20),
        name="whiten",
    )(slot, rows, own, other)


def restore_kernel(rank_ref, bins_ref, out_ref, mat_ref):
    slots, half_rows, bin_width = bins_ref.shape
    rows, chunk = out_ref.shape
    units = bin_width // LANES
    his = mat_ref.shape[0] // rows

    @pl.when(pl.program_id(0) == 0)
    def _():
        for h in range(his):
            for side in range(LO // LANES):
                pair, u = divmod(h * (LO // LANES) + side, units)
                lanes = slice(u * LANES, (u + 1) * LANES)
                both = jnp.concatenate([bins_ref[2 * pair, :, lanes], bins_ref[2 * pair + 1, :, lanes]], axis=0)
                mat_ref[h * rows : (h + 1) * rows, side * LANES : (side + 1) * LANES] = both

    rank = rank_ref[...]
    hi = rank // LO
    lo = rank - hi * LO
    lo_hot = jnp.where(iota((LO, chunk), 0) == lo, 1.0, 0.0).astype(BF16)
    got = dot(mat_ref[...], lo_hot)
    hi_rows = jnp.broadcast_to(hi, (8, chunk))
    for s in range(0, rows, 8):
        value = got[s : s + 8]
        for h in range(1, his):
            value = jnp.where(hi_rows == h, got[h * rows + s : h * rows + s + 8], value)
        out_ref[s : s + 8, :] = value.astype(BF16)


def restore(rank, bins, chunk=1024):
    slots, half_rows, bin_width = bins.shape
    width = rank.shape[1]
    rows = 2 * half_rows
    return pl.pallas_call(
        restore_kernel,
        grid=(width // chunk,),
        in_specs=[
            pl.BlockSpec((1, chunk), lambda i: (0, i)),
            pl.BlockSpec(bins.shape, lambda i: (0, 0, 0)),
        ],
        out_specs=pl.BlockSpec((rows, chunk), lambda i: (0, i)),
        out_shape=jax.ShapeDtypeStruct((rows, width), BF16),
        scratch_shapes=[pltpu.VMEM((rows * (width // LO), LO), BF16)],
        compiler_params=pltpu.CompilerParams(vmem_limit_bytes=48 << 20),
        name="restore",
    )(rank, bins)


def partner(x):
    return lax.ppermute(x, "samples_2", [(0, 1), (1, 0)])


def body(observed, labels, comp_sizes):
    row_local, width_local = observed.shape
    slots = comp_sizes.shape[0]
    groups = lax.axis_size("groups")
    entries = row_local * lax.axis_size(SAMPLES) * width_local * groups
    slot = lax.axis_index(SAMPLES).astype(jnp.int32).reshape(1)
    message, rank = partition(comp_sizes, labels, observed)
    received = lax.all_to_all(message, SAMPLES, split_axis=0, concat_axis=0, tiled=True)
    energy = jnp.sum(received[:, :, CMAX + LANES :].astype(F32), axis=(0, 1)).reshape(1, LANES)
    shifted = [
        lax.ppermute(energy, "groups", [(i, (i + k) % groups) for i in range(groups)]) for k in range(1, groups)
    ]
    energy = sum(shifted, energy)
    rows = received.reshape(slots * (row_local // 2), -1)
    own = component_inverse(slot, comp_sizes, energy, rows, partner(rows), entries)
    mapped = whiten(slot, rows, own, partner(own))
    mapped = mapped.reshape(slots, row_local // 2, -1)
    returned = lax.all_to_all(mapped, SAMPLES, split_axis=0, concat_axis=0, tiled=True)
    return restore(rank, returned)


def solution(mesh):
    finer = Mesh(
        mesh.devices.reshape(8, 4, 2, mesh.shape["groups"]),
        ("samples_0", "samples_1", "samples_2", "groups"),
    )
    in_specs = (P(SAMPLES, "groups"), P("groups"), P("groups"))
    out_specs = P(SAMPLES, "groups")
    return jax.shard_map(body, mesh=finer, in_specs=in_specs, out_specs=out_specs, check_vma=False)
```

time: 432 us -> 123 us (0.28); the launches traced: 423 us -> 123 us
  local copies, waits for them, and re-layouts: 257 us -> 2.63 us
  Pallas kernels: 0 us -> 47.4 us
  other arithmetic: 33.3 us -> 0.09 us
  matrix products: 26 us -> 0 us
  waiting for transfers between devices: 21.7 us -> 4.54 us
  blocking collectives: 72 us -> 61.5 us
    gather x3 -> x0, local copies, waits for them, and re-layouts: 148 us -> none  [the longest x2 75.7 us: body(): tight = observed[:, sort_order]]
    scatter x1 -> x0, local copies, waits for them, and re-layouts: 75.5 us -> none  [body(): rank = jnp.zeros((width_local,), jnp.int32).at[sort_order].set(jnp.arange...]
    pallas_call x0 -> x4, Pallas kernels: none -> 47.4 us  [the longest x1 19.8 us: partition(): pl.pallas_call(partition_kernel, grid=(width // chunk,), in_specs=[pl.Blo...]
    psum x4 -> x0, blocking collectives: 38.7 us -> none  [one_axis_at_a_time(): x = lax.psum(x, axis)]
    all_to_all x1 -> x2, blocking collectives: 33.3 us -> 61.5 us  [the longest x1 35.7 us: body(): lax.all_to_all(message, SAMPLES, split_axis=0, concat_axis=0, tiled=True)]
    dot_general x12 -> x0, matrix products: 26 us -> none  [the longest x5 12.6 us: newton_batch(): jnp.einsum('kab,kbc->kac', matrices, current, precision=lax.Precision.HIG...]
    all_to_all x1 -> x0, waiting for transfers between devices: 20.3 us -> none  [body(): lax.all_to_all(mapped[:, None, :], SAMPLES, split_axis=0, concat_axis=1,...]
    select_n x2 -> x0, other arithmetic: 12.6 us -> none  [the longest x1 12.5 us: body(): return jnp.take(ordered, rank, axis=1)]
  transfers between devices with their start and end apart: 3 -> 5, of which waited for: 2 -> 3; matrix products, arithmetic and copies ran while one was open for 20% -> 0% of each run, Pallas kernels for 0% -> 0%
where the time goes in v1:
time: 123 us
  blocking collectives  61.5 us (50%)
  Pallas kernels  47.4 us (39%)
  starting transfers between devices  7.05 us (6%)
  waiting for transfers between devices  4.54 us (4%)
  local copies, waits for them, and re-layouts  2.63 us (2%)
    all_to_all x1, blocking collectives, body(): lax.all_to_all(message, SAMPLES, split_axis=0, concat_axis=0, tiled=True)  35.7 us
    all_to_all x1, blocking collectives, body(): lax.all_to_all(mapped, SAMPLES, split_axis=0, concat_axis=0, tiled=True)  25.8 us
    pallas_call x1, Pallas kernels, partition(): pl.pallas_call(partition_kernel, grid=(width // chunk,), in_specs=[pl.Blo...  19.8 us
    pallas_call x1, Pallas kernels, restore(): pl.pallas_call(restore_kernel, grid=(width // chunk,), in_specs=[pl.Block...  18.2 us
    pallas_call x1, Pallas kernels, component_inverse(): pl.pallas_call(functools.partial(inverse_kernel, entries=entries), grid=(...  8.63 us
    ppermute x3, starting transfers between devices, body(): lax.ppermute(energy, 'groups', [(i, (i + k) % groups) for i in range(grou...  4.29 us
    ppermute x3, waiting for transfers between devices, body(): lax.ppermute(energy, 'groups', [(i, (i + k) % groups) for i in range(grou...  3 us
    ppermute x2, starting transfers between devices, partner(): return lax.ppermute(x, 'samples_2', [(0, 1), (1, 0)])  2.77 us
  transfers between devices with their start and end apart: 5, of which 3 were waited for; matrix products, arithmetic and copies ran while one was open for 0% of the time, Pallas kernels for 0%

profile of v1, /device:TPU:1, one launch (start us, length us, event | category | flops | bytes accessed | tf_op | source)
XLA Modules:
  0.0 123.2 jit_solution(12094535964325111856)
XLA Ops:
  0.0 0.0 copy-start.2
  0.0 0.7 copy-done.2
  0.7 0.0 copy-start
  0.7 1.1 copy-done
  1.7 0.0 copy-start.1
  1.7 0.9 copy-done.1
  2.6 19.8 %partition.1 = (bf16[64,8,768]{2,1,0:T(8,128)(2,1)S(1)}, s32[1,20480]{1,0:T(1,128)S(1)}) custom-call(s32[1,64]{1,0:T(1,128)S(1)} %bitcast.12, s32[1,20480]{1,0:T(1,128)S(1)} %bitcast.11, bf16[16,20480]{1,0:T(8,128)(2,1)S(1)} %copy-done), custom_call_target="tpu_custom_call" | custom-call | tf_op jit(solution)/shard_map/partition/pallas_call | solution.py:108
  22.5 35.7 %all_to_all.10 = bf16[64,8,768]{2,1,0:T(8,128)(2,1)S(1)} all-to-all(bf16[64,8,768]{2,1,0:T(8,128)(2,1)S(1)} %get-tuple-element.8), channel_id=1, replica_groups=mesh['samples_0'=8,'samples_1'=4,'samples_2'=2,'groups'=4] {'samples_0',..., dimensions={0} | all-to-all | bytes 1572864 | tf_op jit(solution)/shard_map/all_to_all | solution.py:291
  58.2 1.0 collective-permute-start.3
  59.2 0.1 convert_reduce_fusion
  59.2 2.8 %collective-permute-start.1 = (f32[1,128]{1,0:T(1,128)S(1)}, f32[1,128]{1,0:T(1,128)S(1)}, u32[]{:S(2)}, u32[]{:S(2)}) collective-permute-start(f32[1,128]{1,0:T(1,128)S(1)} %bitcast.13), channel_id=1, source_target_pairs={{0,2},{1,3},{2,0},{3,1},{4,6},{5,7},{6,4},{7,5},{8,10},{9,11},{10,... | collective-permute-start | bytes 1544 | tf_op jit(solution)/shard_map/ppermute | solution.py:294
  62.1 0.9 collective-permute-start.2
  62.9 0.6 collective-permute-start
  63.5 0.0 collective-permute-done.1
  63.5 0.9 collective-permute-done.2
  64.5 2.1 %collective-permute-done = f32[1,128]{1,0:T(1,128)S(1)} collective-permute-done((f32[1,128]{1,0:T(1,128)S(1)}, f32[1,128]{1,0:T(1,128)S(1)}, u32[]{:S(2)}, u32[]{:S(2)}) %collective-permute-start) | collective-permute-done | bytes 544 | tf_op jit(solution)/shard_map/ppermute | solution.py:294
  66.5 0.0 collective-permute-done.3.other_ref
  66.5 8.6 %component_inverse.1.own_ref = bf16[512,512]{1,0:T(8,128)(2,1)S(1)} custom-call(s32[1]{0:T(128)} %bitcast.2.slot_ref, s32[64]{0:T(128)S(1)} %copy-done.2, f32[1,128]{1,0:T(1,128)S(1)} %add_add_fusion.energy_ref, bf16[512,768]{1,0:T(8,128)(2,1)S(1)} %bitcast.8, bf16[512,768]{1,0:T(8,128)(2,1)S(1)} %collective-permute-done.3.other_ref), custom_call_target="tpu_custom_call" | custom-call | tf_op jit(solution)/shard_map/component_inverse/pallas_call | solution.py:183
  75.2 1.8 %collective-permute-start.4 = (bf16[512,512]{1,0:T(8,128)(2,1)S(1)}, bf16[512,512]{1,0:T(8,128)(2,1)S(1)}, u32[]{:S(2)}, u32[]{:S(2)}) collective-permute-start(bf16[512,512]{1,0:T(8,128)(2,1)S(1)} %component_inverse.1.own_ref), channel_id=1, source_target_pairs={{0,4},{4,0},{1,5},{5,1},{2,6},{6,2},{3,7},{7,3},{8,12},{12,8},{9,1... | collective-permute-start | bytes 1572872 | tf_op jit(solution)/shard_map/ppermute | solution.py:281
  77.0 1.5 %collective-permute-done.4.other_ref = bf16[512,512]{1,0:T(8,128)(2,1)S(1)} collective-permute-done((bf16[512,512]{1,0:T(8,128)(2,1)S(1)}, bf16[512,512]{1,0:T(8,128)(2,1)S(1)}, u32[]{:S(2)}, u32[]{:S(2)}) %collective-permute-start.4) | collective-permute-done | bytes 524320 | tf_op jit(solution)/shard_map/ppermute | solution.py:281
  78.5 0.7 whiten.1
  79.2 25.8 %all_to_all.11.bins_ref = bf16[64,8,640]{2,1,0:T(8,128)(2,1)S(1)} all-to-all(bf16[64,8,640]{2,1,0:T(8,128)(2,1)S(1)} %bitcast.10), channel_id=1, replica_groups=mesh['samples_0'=8,'samples_1'=4,'samples_2'=2,'groups'=4] {'samples_0',..., dimensions={0} | all-to-all | bytes 1310720 | tf_op jit(solution)/shard_map/all_to_all | solution.py:301
  105.0 18.2 %restore.1 = bf16[16,20480]{1,0:T(8,128)(2,1)} custom-call(s32[1,20480]{1,0:T(1,128)S(1)} %get-tuple-element.7.rank_ref, bf16[64,8,640]{2,1,0:T(8,128)(2,1)S(1)} %all_to_all.11.bins_ref), custom_call_target="tpu_custom_call" | custom-call | tf_op jit(solution)/shard_map/restore/pallas_call | solution.py:265
  (1 shorter events, 0.0 us)
Async XLA Ops:
  0.0 0.7 copy-start.2
  0.7 1.1 copy-start
  1.7 0.9 copy-start.1
  58.2 8.4 %collective-permute-start.3 = (bf16[512,768]{1,0:T(8,128)(2,1)S(1)}, bf16[512,768]{1,0:T(8,128)(2,1)S(1)}, u32[]{:S(2)}, u32[]{:S(2)}) collective-permute-start(bf16[512,768]{1,0:T(8,128)(2,1)S(1)} %bitcast.7), channel_id=1, source_target_pairs={{0,4},{4,0},{1,5},{5,1},{2,6},{6,2},{3,7},{7,3},{8,12},{12,8},{9,1... | collective-permute-start | bytes 2359304 | tf_op jit(solution)/shard_map/ppermute | solution.py:281
  59.2 4.3 %collective-permute-start.1 = (f32[1,128]{1,0:T(1,128)S(1)}, f32[1,128]{1,0:T(1,128)S(1)}, u32[]{:S(2)}, u32[]{:S(2)}) collective-permute-start(f32[1,128]{1,0:T(1,128)S(1)} %bitcast.13), channel_id=1, source_target_pairs={{0,2},{1,3},{2,0},{3,1},{4,6},{5,7},{6,4},{7,5},{8,10},{9,11},{10,... | collective-permute-start | bytes 1544 | tf_op jit(solution)/shard_map/ppermute | solution.py:294
  62.1 2.4 %collective-permute-start.2 = (f32[1,128]{1,0:T(1,128)S(1)}, f32[1,128]{1,0:T(1,128)S(1)}, u32[]{:S(2)}, u32[]{:S(2)}) collective-permute-start(f32[1,128]{1,0:T(1,128)S(1)} %bitcast.14), channel_id=1, source_target_pairs={{0,3},{1,0},{2,1},{3,2},{4,7},{5,4},{6,5},{7,6},{8,11},{9,8},{10,9... | collective-permute-start | bytes 1544 | tf_op jit(solution)/shard_map/ppermute | solution.py:294
  62.9 3.6 %collective-permute-start = (f32[1,128]{1,0:T(1,128)S(1)}, f32[1,128]{1,0:T(1,128)S(1)}, u32[]{:S(2)}, u32[]{:S(2)}) collective-permute-start(f32[1,128]{1,0:T(1,128)S(1)} %bitcast.15), channel_id=1, source_target_pairs={{0,1},{1,2},{2,3},{3,0},{4,5},{5,6},{6,7},{7,4},{8,9},{9,10},{10,1... | collective-permute-start | bytes 1544 | tf_op jit(solution)/shard_map/ppermute | solution.py:294
  75.2 3.3 %collective-permute-start.4 = (bf16[512,512]{1,0:T(8,128)(2,1)S(1)}, bf16[512,512]{1,0:T(8,128)(2,1)S(1)}, u32[]{:S(2)}, u32[]{:S(2)}) collective-permute-start(bf16[512,512]{1,0:T(8,128)(2,1)S(1)} %component_inverse.1.own_ref), channel_id=1, source_target_pairs={{0,4},{4,0},{1,5},{5,1},{2,6},{6,2},{3,7},{7,3},{8,12},{12,8},{9,1... | collective-permute-start | bytes 1572872 | tf_op jit(solution)/shard_map/ppermute | solution.py:281
